TPU v7x, 256 devices: a whole 4x4x8 slice. The times are simulated.
256 devices in a mesh: wide: 32 (over z, y), slab: 8 (over x, core).
Axes of the slice: x: 4, y: 4, z: 8, core: 2. Of those that a mesh axis runs over, the one named last changes fastest.
Arguments:
- thermal_state: float32 [32, 128, 32, 1024], P('wide', 'slab'), may hold values from -5 to 5
- thermal_spreading_rate: bfloat16 [32, 128, 32, 1024], P('wide', 'slab'), may hold values from 0.5 to 1.5
- flow_speed_vector: bfloat16 [3, 32, 128, 32, 1024], P(None, 'wide', 'slab'), may hold values from -0.796875 to 0.796875
- interface_guess: float32 [32, 2048], P('wide', 'slab'), may hold values from -4 to 4
- partner_facing_rows: int32 [32, 2048], P('wide', 'slab'), may hold values from 0 to 2047, each once within a row
- mismatch_change_matrix: float32 [32, 2048, 128], P('wide', 'slab'), may hold values from -5 to 5
- output_change_matrix: float32 [32, 2048, 128], P('wide', 'slab'), may hold values from -1.8 to 1.8
Outputs:
- temperature_out: float32 [32, 128, 32, 1024], P('wide', 'slab')
- updated_interface_guess: float32 [32, 2048], P('wide', 'slab')
- unitary_basis_factor: float32 [32, 2048, 128], P('wide', 'slab')
Inputs may be any that keep to these rules, and one draw needn't show every extreme that they name: `partner_facing_rows`: each partition's rows of matching are a permutation of its partner's interface rows.
All inputs are finite; a program needn't handle non-finite values.
Results may differ from a plain program's by a relative error of at most 0.0003.
Values may be sent and summed in bfloat16 or wider, within the bound.
No kernel may reach another device: no remote copies, remote signals or barrier semaphores. Data moves between devices by JAX's collectives and lax.ppermute only.
A program may use at most 64 MiB of HBM per device.

v0:
```python
import math
import jax
import jax.numpy as jnp
from jax import lax
from jax.sharding import PartitionSpec as P

INTERFACE_STRIP = 64
SWEEPS = 4
STEP_SIZE = 0.11


def padded(cells, sides, width):
    for axis, dim in sides:
        count = lax.axis_size(axis)
        ends = count - 1
        head = lax.slice_in_dim(cells, 0, width, axis=dim)
        tail = lax.slice_in_dim(cells, cells.shape[dim] - width, cells.shape[dim], axis=dim)
        cells = jnp.concatenate(
            [
                lax.ppermute(tail, axis, [(i, (i + 1) % count) for i in range(ends)]),
                cells,
                lax.ppermute(head, axis, [((i + 1) % count, i) for i in range(ends)]),
            ],
            axis=dim,
        )
    return cells


def partner(value, axis, stride):
    mask = 2**stride
    pairs = [(source, source ^ mask) for source in range(lax.axis_size(axis))]
    return lax.ppermute(value, axis, pairs)


def gather_sum(value, axes):
    count = lax.axis_size(axes)
    copies = jnp.broadcast_to(value[None], (count, *value.shape))
    return jnp.sum(lax.all_to_all(copies, axes, 0, 0, tiled=True), axis=0)


def sum_everywhere(square):
    rows = square.shape[0] // lax.axis_size("slab")
    blocks = square.reshape(-1, rows, square.shape[1])
    mine = jnp.sum(lax.all_to_all(blocks, "slab", 0, 0, tiled=True), axis=0)
    mine = gather_sum(mine, "wide")
    copies = jnp.broadcast_to(mine[None], blocks.shape)
    return lax.all_to_all(copies, "slab", 0, 0, tiled=True).reshape(square.shape)


def surround_wrapper(block_rows, mirror_layer):
    bottom = jnp.zeros((block_rows.shape[0], 1, block_rows.shape[2]), block_rows.dtype)
    stacked = jnp.concatenate([bottom, block_rows, mirror_layer[:, None, :]], axis=1)
    return jnp.pad(stacked, ((0, 0), (0, 0), (1, 1)))


def march_forward(bordered_array, diffuse_subdomain, subdomain_flow_speed):
    centre = bordered_array[1:-1, 1:-1, 1:-1]
    plus_first = bordered_array[2:, 1:-1, 1:-1]
    minus_first = bordered_array[:-2, 1:-1, 1:-1]
    plus_second = bordered_array[1:-1, 2:, 1:-1]
    minus_second = bordered_array[1:-1, :-2, 1:-1]
    plus_third = bordered_array[1:-1, 1:-1, 2:]
    minus_third = bordered_array[1:-1, 1:-1, :-2]
    spread = (
        plus_first
        + minus_first
        + plus_second
        + minus_second
        + plus_third
        + minus_third
        - 6.0 * centre
    )
    carried = 0.5 * (
        subdomain_flow_speed[0].astype(jnp.float32) * (plus_first - minus_first)
        + subdomain_flow_speed[1].astype(jnp.float32) * (plus_second - minus_second)
        + subdomain_flow_speed[2].astype(jnp.float32) * (plus_third - minus_third)
    )
    return centre + STEP_SIZE * (diffuse_subdomain.astype(jnp.float32) * spread - carried)


def shards(
    thermal_state,
    thermal_spreading_rate,
    flow_speed_vector,
    interface_guess,
    partner_facing_rows,
    mismatch_change_matrix,
    output_change_matrix,
):
    subdomain_thermal_state = thermal_state[0]
    diffuse_subdomain = thermal_spreading_rate[0]
    subdomain_flow_speed = flow_speed_vector[:, 0]
    layer_stack = subdomain_thermal_state.shape[0]
    vertical_extent = subdomain_thermal_state.shape[1]
    rows_dev = interface_guess.shape[1]
    mirror_layer = jnp.repeat(interface_guess[0].reshape(layer_stack, -1), INTERFACE_STRIP, axis=1)
    panel = mismatch_change_matrix[0]
    gram_local = lax.dot_general(
        panel,
        panel,
        (((0,), (0,)), ((), ())),
        precision=lax.Precision.HIGHEST,
        preferred_element_type=jnp.float32,
    )
    ghost_padded = jnp.pad(mirror_layer, ((1, 1), (0, 0)))
    for sweep in range(SWEEPS):
        widened_array = padded(subdomain_thermal_state, (("slab", 0),), 1)
        subdomain_thermal_state = march_forward(
            surround_wrapper(widened_array, ghost_padded), diffuse_subdomain, subdomain_flow_speed
        )
    face_means = jnp.mean(
        subdomain_thermal_state[:, vertical_extent - 1, :].reshape(
            layer_stack, -1, INTERFACE_STRIP
        ),
        axis=2,
    )
    face_means = face_means.reshape(1, rows_dev)
    top_bit = lax.axis_size("wide").bit_length() - 2
    partner_own = partner(face_means, "wide", top_bit)
    partner_all = lax.all_gather(partner_own, "slab", axis=1, tiled=True)
    tilde = jnp.take(partner_all[0], partner_facing_rows[0], axis=0)
    resid = tilde - interface_guess[0]
    proj_local = jnp.dot(
        resid, panel, precision=lax.Precision.HIGHEST, preferred_element_type=jnp.float32
    )
    gram_matrix = sum_everywhere(gram_local)
    projection = gather_sum(proj_local, ("wide", "slab"))
    lower_factor = jnp.linalg.cholesky(gram_matrix)
    half_solve = lax.linalg.triangular_solve(
        lower_factor, projection[:, None], left_side=True, lower=True
    )
    coefficients = -lax.linalg.triangular_solve(
        lower_factor, half_solve, left_side=True, lower=True, transpose_a=True
    )[:, 0]
    update = jnp.dot(
        output_change_matrix[0],
        coefficients,
        precision=lax.Precision.HIGHEST,
        preferred_element_type=jnp.float32,
    )
    updated_interface_guess = tilde + update
    total_rows = rows_dev * lax.axis_size("slab") * lax.axis_size("wide")
    scaled = lax.linalg.triangular_solve(
        lower_factor, panel, left_side=False, lower=True, transpose_a=True
    )
    unitary_basis_factor = math.sqrt(total_rows) * scaled
    return (
        subdomain_thermal_state[None],
        updated_interface_guess[None],
        unitary_basis_factor[None],
    )


def solution(mesh):
    return jax.shard_map(
        shards,
        mesh=mesh,
        in_specs=(
            P("wide", "slab", None, None),
            P("wide", "slab", None, None),
            P(None, "wide", "slab", None, None),
            P("wide", "slab"),
            P("wide", "slab"),
            P("wide", "slab", None),
            P("wide", "slab", None),
        ),
        out_specs=(P("wide", "slab", None, None), P("wide", "slab"), P("wide", "slab", None)),
        check_vma=False,
    )
```

profile of v0, /device:TPU:1, one launch (start us, length us, event | category | flops | bytes accessed | tf_op | source)
XLA Modules:
  0.0 155.6 jit_solution(3249432732262084621)
XLA Ops:
  1.7 5.1 %collective-permute-start = (f32[1,32,1024]{2,1,0:T(8,128)S(1)}, f32[1,32,1024]{2,1,0:T(8,128)S(1)}, u32[]{:S(2)}, u32[]{:S(2)}) collective-permute-start(f32[1,32,1024]{2,1,0:T(8,128)S(1)} %get-tuple-element.22), channel_id=1, source_target_pairs={{1,0},{2,1},{3,2},{4,3},{5,4},{6,5},{7,6},{9,8},{10,9},{11,10},{12... | collective-permute-start | bytes 393224 | tf_op jit(solution)/shard_map/ppermute | solution.py:22
  6.8 1.9 %collective-permute-start.1 = (f32[1,32,1024]{2,1,0:T(8,128)S(1)}, f32[1,32,1024]{2,1,0:T(8,128)S(1)}, u32[]{:S(2)}, u32[]{:S(2)}) collective-permute-start(f32[1,32,1024]{2,1,0:T(8,128)S(1)} %get-tuple-element.21), channel_id=1, source_target_pairs={{0,1},{1,2},{2,3},{3,4},{4,5},{5,6},{6,7},{8,9},{9,10},{10,11},{11... | collective-permute-start | bytes 393224 | tf_op jit(solution)/shard_map/ppermute | solution.py:20
  9.3 1.3 reduce.12
  11.7 2.3 %pad_maximum_fusion.3 = f32[18,34,1024]{2,1,0:T(8,128)S(1)} fusion(f32[18,1,1024]{2,1,0:T(1,128)S(1)} %broadcast_in_dim.48, f32[1,32,1024]{2,1,0:T(8,128)S(1)} %collective-permute-done, f32[16,32,1024]{2,1,0:T(8,128)} %bitcast.102, f32[1,32,1024]{2,1,0:T(8,128)} %copy-done.15, f32[34]{0:T(128)S(1)} %pad.74.clone), kind=kLoop, calls=%fused_computation.4 | loop fusion | flops 2506752 | bytes 4939912 | tf_op jit(solution)/shard_map/concatenate | solution.py:52
  14.6 7.1 %fusion.2 = f32[16,32,1024]{2,1,0:T(8,128)S(1)} fusion(f32[16,32,1024]{2,1,0:T(8,128)} %bitcast.103, f32[18,34,1024]{2,1,0:T(8,128)S(1)} %pad_maximum_fusion.3, f32[1,32,1024]{2,1,0:T(8,128)} %copy-done.14, f32[1,32,1024]{2,1,0:T(8,128)S(1)} %copy-done.16, f32[18,1,1024]{2,1,0:T(1,128)S(1)} %broadcast_in_dim.48, bf16[1,16,32,1024]{3,2,1,0:T(8,128)(2,1)S(1)} %copy-done.8, ...), kind=kLoop, calls=%fused_computation.35 | loop fusion | flops 18874368 | bytes 11231232 | tf_op jit(solution)/shard_map/add | solution.py:78
  21.7 1.3 copy-done.6
  23.7 2.4 %collective-permute-start.2 = (f32[1,32,1024]{2,1,0:T(8,128)}, f32[1,32,1024]{2,1,0:T(8,128)}, u32[]{:S(2)}, u32[]{:S(2)}) collective-permute-start(f32[1,32,1024]{2,1,0:T(8,128)} %get-tuple-element.20), channel_id=1, source_target_pairs={{1,0},{2,1},{3,2},{4,3},{5,4},{6,5},{7,6},{9,8},{10,9},{11,10},{12... | collective-permute-start | bytes 393224 | tf_op jit(solution)/shard_map/ppermute | solution.py:22
  26.1 3.5 %collective-permute-start.3 = (f32[1,32,1024]{2,1,0:T(8,128)}, f32[1,32,1024]{2,1,0:T(8,128)}, u32[]{:S(2)}, u32[]{:S(2)}) collective-permute-start(f32[1,32,1024]{2,1,0:T(8,128)} %get-tuple-element.19), channel_id=1, source_target_pairs={{0,1},{1,2},{2,3},{3,4},{4,5},{5,6},{6,7},{8,9},{9,10},{10,11},{11... | collective-permute-start | bytes 393224 | tf_op jit(solution)/shard_map/ppermute | solution.py:20
  31.9 2.2 %pad_maximum_fusion.2 = f32[18,34,1024]{2,1,0:T(8,128)S(1)} fusion(f32[18,1,1024]{2,1,0:T(1,128)S(1)} %broadcast_in_dim.48, f32[1,32,1024]{2,1,0:T(8,128)} %collective-permute-done.2, f32[16,32,1024]{2,1,0:T(8,128)} %copy-done.6, f32[1,32,1024]{2,1,0:T(8,128)} %collective-permute-done.3, f32[34]{0:T(128)S(1)} %pad.74.clone), kind=kLoop, calls=%fused_computation.3 | loop fusion | flops 2506752 | bytes 4939912 | tf_op jit(solution)/shard_map/concatenate | solution.py:52
  34.1 4.7 %fusion.5 = f32[16,32,1024]{2,1,0:T(8,128)S(1)} fusion(f32[16,32,1024]{2,1,0:T(8,128)S(1)} %copy-done.7, f32[18,34,1024]{2,1,0:T(8,128)S(1)} %pad_maximum_fusion.2, f32[1,32,1024]{2,1,0:T(8,128)} %collective-permute-done.2, f32[1,32,1024]{2,1,0:T(8,128)} %collective-permute-done.3, f32[18,1,1024]{2,1,0:T(1,128)S(1)} %broadcast_in_dim.48, ...), kind=kLoop, calls=%fused_computation.38 | loop fusion | flops 18874368 | bytes 11231232 | tf_op jit(solution)/shard_map/add | solution.py:78
  38.9 1.3 copy-done.4
  40.9 1.9 %collective-permute-start.4 = (f32[1,32,1024]{2,1,0:T(8,128)}, f32[1,32,1024]{2,1,0:T(8,128)}, u32[]{:S(2)}, u32[]{:S(2)}) collective-permute-start(f32[1,32,1024]{2,1,0:T(8,128)} %get-tuple-element.18), channel_id=1, source_target_pairs={{1,0},{2,1},{3,2},{4,3},{5,4},{6,5},{7,6},{9,8},{10,9},{11,10},{12... | collective-permute-start | bytes 393224 | tf_op jit(solution)/shard_map/ppermute | solution.py:22
  42.8 4.4 %collective-permute-start.5 = (f32[1,32,1024]{2,1,0:T(8,128)}, f32[1,32,1024]{2,1,0:T(8,128)}, u32[]{:S(2)}, u32[]{:S(2)}) collective-permute-start(f32[1,32,1024]{2,1,0:T(8,128)} %get-tuple-element.17), channel_id=1, source_target_pairs={{0,1},{1,2},{2,3},{3,4},{4,5},{5,6},{6,7},{8,9},{9,10},{10,11},{11... | collective-permute-start | bytes 393224 | tf_op jit(solution)/shard_map/ppermute | solution.py:20
  48.1 3.7 %all-to-all-start = ((f32[8,16,128]{2,1,0:T(8,128)}), f32[8,16,128]{2,1,0:T(8,128)S(1)}, u32[]{:S(2)}, u32[]{:S(2)}) async-start(f32[8,16,128]{2,1,0:T(8,128)} %fusion.37), calls=%async_computation | async-start | bytes 131072 | tf_op jit(solution)/shard_map/all_to_all | solution.py:44
  51.8 2.3 %pad_maximum_fusion.1 = f32[18,34,1024]{2,1,0:T(8,128)S(1)} fusion(f32[18,1,1024]{2,1,0:T(1,128)S(1)} %broadcast_in_dim.48, f32[1,32,1024]{2,1,0:T(8,128)} %collective-permute-done.4, f32[16,32,1024]{2,1,0:T(8,128)} %copy-done.4, f32[1,32,1024]{2,1,0:T(8,128)} %collective-permute-done.5, f32[34]{0:T(128)S(1)} %pad.74.clone), kind=kLoop, calls=%fused_computation.2 | loop fusion | flops 2506752 | bytes 4939912 | tf_op jit(solution)/shard_map/concatenate | solution.py:52
  54.4 4.7 %fusion.8 = f32[16,32,1024]{2,1,0:T(8,128)S(1)} fusion(f32[16,32,1024]{2,1,0:T(8,128)S(1)} %copy-done.5, f32[18,34,1024]{2,1,0:T(8,128)S(1)} %pad_maximum_fusion.1, f32[1,32,1024]{2,1,0:T(8,128)} %collective-permute-done.4, f32[1,32,1024]{2,1,0:T(8,128)} %collective-permute-done.5, f32[18,1,1024]{2,1,0:T(1,128)S(1)} %broadcast_in_dim.48, ...), kind=kLoop, calls=%fused_computation.41 | loop fusion | flops 18874368 | bytes 11231232 | tf_op jit(solution)/shard_map/add | solution.py:78
  59.1 1.3 copy-done.2
  61.1 1.9 %collective-permute-start.6 = (f32[1,32,1024]{2,1,0:T(8,128)}, f32[1,32,1024]{2,1,0:T(8,128)}, u32[]{:S(2)}, u32[]{:S(2)}) collective-permute-start(f32[1,32,1024]{2,1,0:T(8,128)} %get-tuple-element.16), channel_id=1, source_target_pairs={{1,0},{2,1},{3,2},{4,3},{5,4},{6,5},{7,6},{9,8},{10,9},{11,10},{12... | collective-permute-start | bytes 393224 | tf_op jit(solution)/shard_map/ppermute | solution.py:22
  63.0 3.6 %collective-permute-start.7 = (f32[1,32,1024]{2,1,0:T(8,128)}, f32[1,32,1024]{2,1,0:T(8,128)}, u32[]{:S(2)}, u32[]{:S(2)}) collective-permute-start(f32[1,32,1024]{2,1,0:T(8,128)} %get-tuple-element.15), channel_id=1, source_target_pairs={{0,1},{1,2},{2,3},{3,4},{4,5},{5,6},{6,7},{8,9},{9,10},{10,11},{11... | collective-permute-start | bytes 393224 | tf_op jit(solution)/shard_map/ppermute | solution.py:20
  68.0 11.3 %all-to-all-start.1 = ((f32[32,16,128]{2,1,0:T(8,128)}), f32[32,16,128]{2,1,0:T(8,128)}, u32[]{:S(2)}, u32[]{:S(2)}) async-start(f32[32,16,128]{2,1,0:T(8,128)} %broadcast_in_dim.51), calls=%async_computation.1 | async-start | bytes 524288 | tf_op jit(solution)/shard_map/all_to_all | solution.py:38
  79.4 2.3 %pad_maximum_fusion = f32[18,34,1024]{2,1,0:T(8,128)S(1)} fusion(f32[18,1,1024]{2,1,0:T(1,128)S(1)} %broadcast_in_dim.48, f32[1,32,1024]{2,1,0:T(8,128)} %collective-permute-done.6, f32[16,32,1024]{2,1,0:T(8,128)} %copy-done.2, f32[1,32,1024]{2,1,0:T(8,128)} %collective-permute-done.7, f32[34]{0:T(128)} %copy-done.20), kind=kLoop, calls=%fused_computation.1 | loop fusion | flops 2506752 | bytes 4939912 | tf_op jit(solution)/shard_map/concatenate | solution.py:52
  81.9 4.7 %fusion.11 = f32[16,32,1024]{2,1,0:T(8,128)S(1)} fusion(f32[16,32,1024]{2,1,0:T(8,128)S(1)} %copy-done.3, f32[18,34,1024]{2,1,0:T(8,128)S(1)} %pad_maximum_fusion, f32[1,32,1024]{2,1,0:T(8,128)} %collective-permute-done.6, f32[1,32,1024]{2,1,0:T(8,128)} %collective-permute-done.7, f32[18,1,1024]{2,1,0:T(1,128)S(1)} %broadcast_in_dim.48, ...), kind=kLoop, calls=%fused_computation.44 | loop fusion | flops 18874368 | bytes 11231232 | tf_op jit(solution)/shard_map/add | solution.py:78
  86.7 1.3 copy-done.12
  88.5 5.3 %collective-permute-start.8 = (f32[1,256]{1,0:T(1,128)S(1)}, f32[1,256]{1,0:T(1,128)S(1)}, u32[]{:S(2)}, u32[]{:S(2)}) collective-permute-start(f32[1,256]{1,0:T(1,128)S(1)} %div.18), channel_id=1, source_target_pairs={{0,128},{8,136},{16,144},{24,152},{32,160},{40,168},{48,176},{56,1... | collective-permute-start | bytes 3080 | tf_op jit(solution)/shard_map/ppermute | solution.py:32
  93.7 1.2 collective-permute-done.8
  95.0 11.7 %all_gather.3 = f32[1,2048]{1,0:T(1,128)S(1)} all-gather(f32[1,256]{1,0:T(1,128)S(1)} %collective-permute-done.8), channel_id=1, replica_groups=mesh['wide'=32,'slab'=8] {'slab'}, dimensions={1}, use_global_device_ids=true | all-gather | bytes 9216 | tf_op jit(solution)/shard_map/all_gather | solution.py:120
  106.6 1.7 %gather_fusion = f32[256]{0:T(256)S(1)} fusion(f32[2048]{0:T(1024)S(1)} %bitcast.101, s32[1024]{0:T(1024)S(1)} %pad_clamp_fusion), kind=kCustom, calls=%fused_computation | custom fusion | bytes 3072 | tf_op jit(solution)/shard_map/jit(_take)/gather | solution.py:121
  110.0 3.4 %all-to-all-start.2 = ((f32[8,16,128]{2,1,0:T(8,128)}), f32[8,16,128]{2,1,0:T(8,128)S(1)}, u32[]{:S(2)}, u32[]{:S(2)}) async-start(f32[8,16,128]{2,1,0:T(8,128)} %broadcast_in_dim.52), calls=%async_computation.2 | async-start | bytes 131072 | tf_op jit(solution)/shard_map/all_to_all | solution.py:47
  113.6 4.7 %all-to-all-done.2 = f32[8,16,128]{2,1,0:T(8,128)S(1)} async-done(((f32[8,16,128]{2,1,0:T(8,128)}), f32[8,16,128]{2,1,0:T(8,128)S(1)}, u32[]{:S(2)}, u32[]{:S(2)}) %all-to-all-start.2) | async-done | bytes 65568 | tf_op jit(solution)/shard_map/all_to_all | solution.py:47
  119.0 11.3 %all-to-all-start.3 = ((f32[256,1,128]{2,1,0:T(1,128)}), f32[256,1,128]{2,1,0:T(1,128)S(1)}, u32[]{:S(2)}, u32[]{:S(2)}) async-start(f32[256,1,128]{2,1,0:T(1,128)} %broadcast_in_dim.54), calls=%async_computation.3 | async-start | bytes 262144 | tf_op jit(solution)/shard_map/all_to_all | solution.py:38
  130.5 11.7 %cholesky.16 = f32[128,128]{1,0:T(8,128)S(1)} custom-call(f32[128,128]{1,0:T(8,128)S(1)} %fusion.45), custom_call_target="Cholesky" | custom-call | tf_op jit(solution)/shard_map/jit(cholesky)/cholesky | solution.py:128
  143.5 9.8 %custom-call.10 = f32[1,128,128]{1,2,0:T(8,128)S(1)} custom-call(f32[1,128,128]{2,1,0:T(8,128)S(1)} %fusion.41), custom_call_target="InvertDiagBlocksLowerTriangular" | custom-call | tf_op jit(solution)/shard_map/triangular_solve | solution.py:132
  (91 shorter events, 16.9 us)
Async XLA Ops:
  0.6 154.2 %copy-start = (f32[1,256,128]{2,1,0:T(8,128)S(1)}, f32[1,256,128]{2,1,0:T(8,128)}, u32[]{:S(2)}) copy-start(f32[1,256,128]{2,1,0:T(8,128)} %param.13) | copy-start | bytes 393220
  1.7 9.3 %collective-permute-start = (f32[1,32,1024]{2,1,0:T(8,128)S(1)}, f32[1,32,1024]{2,1,0:T(8,128)S(1)}, u32[]{:S(2)}, u32[]{:S(2)}) collective-permute-start(f32[1,32,1024]{2,1,0:T(8,128)S(1)} %get-tuple-element.22), channel_id=1, source_target_pairs={{1,0},{2,1},{3,2},{4,3},{5,4},{6,5},{7,6},{9,8},{10,9},{11,10},{12... | collective-permute-start | bytes 393224 | tf_op jit(solution)/shard_map/ppermute | solution.py:22
  6.8 4.2 %collective-permute-start.1 = (f32[1,32,1024]{2,1,0:T(8,128)S(1)}, f32[1,32,1024]{2,1,0:T(8,128)S(1)}, u32[]{:S(2)}, u32[]{:S(2)}) collective-permute-start(f32[1,32,1024]{2,1,0:T(8,128)S(1)} %get-tuple-element.21), channel_id=1, source_target_pairs={{0,1},{1,2},{2,3},{3,4},{4,5},{5,6},{6,7},{8,9},{9,10},{10,11},{11... | collective-permute-start | bytes 393224 | tf_op jit(solution)/shard_map/ppermute | solution.py:20
  11.0 40.8 %copy-start.20 = (f32[34]{0:T(128)}, f32[34]{0:T(128)S(1)}, u32[]{:S(2)}) copy-start(f32[34]{0:T(128)S(1)} %pad.74.clone) | copy-start | bytes 412
  11.7 2.6 %copy-start.1 = (bf16[3,1,16,32,1024]{4,3,2,1,0:T(8,128)(2,1)S(1)}, bf16[3,1,16,32,1024]{4,3,2,1,0:T(8,128)(2,1)}, u32[]{:S(2)}) copy-start(bf16[3,1,16,32,1024]{4,3,2,1,0:T(8,128)(2,1)} %param.9) | copy-start | bytes 9437188
  11.7 2.8 %copy-start.8 = (bf16[1,16,32,1024]{3,2,1,0:T(8,128)(2,1)S(1)}, bf16[1,16,32,1024]{3,2,1,0:T(8,128)(2,1)}, u32[]{:S(2)}) copy-start(bf16[1,16,32,1024]{3,2,1,0:T(8,128)(2,1)} %param.8) | copy-start | bytes 3145732
  11.7 2.8 %copy-start.16 = (f32[1,32,1024]{2,1,0:T(8,128)S(1)}, f32[1,32,1024]{2,1,0:T(8,128)}, u32[]{:S(2)}) copy-start(f32[1,32,1024]{2,1,0:T(8,128)} %copy-done.15) | copy-start | bytes 393220
  14.6 15.1 %copy-start.13 = (f32[1,256,128]{2,1,0:T(8,128)S(1)}, f32[1,256,128]{2,1,0:T(8,128)}, u32[]{:S(2)}) copy-start(f32[1,256,128]{2,1,0:T(8,128)} %param.12) | copy-start | bytes 393220
  21.7 1.3 copy-start.6
  23.7 6.9 %collective-permute-start.2 = (f32[1,32,1024]{2,1,0:T(8,128)}, f32[1,32,1024]{2,1,0:T(8,128)}, u32[]{:S(2)}, u32[]{:S(2)}) collective-permute-start(f32[1,32,1024]{2,1,0:T(8,128)} %get-tuple-element.20), channel_id=1, source_target_pairs={{1,0},{2,1},{3,2},{4,3},{5,4},{6,5},{7,6},{9,8},{10,9},{11,10},{12... | collective-permute-start | bytes 393224 | tf_op jit(solution)/shard_map/ppermute | solution.py:22
  26.1 5.7 %collective-permute-start.3 = (f32[1,32,1024]{2,1,0:T(8,128)}, f32[1,32,1024]{2,1,0:T(8,128)}, u32[]{:S(2)}, u32[]{:S(2)}) collective-permute-start(f32[1,32,1024]{2,1,0:T(8,128)} %get-tuple-element.19), channel_id=1, source_target_pairs={{0,1},{1,2},{2,3},{3,4},{4,5},{5,6},{6,7},{8,9},{9,10},{10,11},{11... | collective-permute-start | bytes 393224 | tf_op jit(solution)/shard_map/ppermute | solution.py:20
  30.4 3.7 %copy-start.7 = (f32[16,32,1024]{2,1,0:T(8,128)S(1)}, f32[16,32,1024]{2,1,0:T(8,128)}, u32[]{:S(2)}) copy-start(f32[16,32,1024]{2,1,0:T(8,128)} %copy-done.6) | copy-start | bytes 6291460
  30.4 3.7 %copy-start.9 = (bf16[1,16,32,1024]{3,2,1,0:T(8,128)(2,1)S(1)}, bf16[1,16,32,1024]{3,2,1,0:T(8,128)(2,1)}, u32[]{:S(2)}) copy-start(bf16[1,16,32,1024]{3,2,1,0:T(8,128)(2,1)} %param.8) | copy-start | bytes 3145732
  34.1 13.1 %copy-start.17 = (f32[1,256,128]{1,2,0:T(8,128)S(1)}, f32[1,256,128]{1,2,0:T(8,128)}, u32[]{:S(2)}) copy-start(f32[1,256,128]{1,2,0:T(8,128)} %copy.21) | copy-start | bytes 393220
  38.8 1.3 copy-start.4
  40.9 10.9 %collective-permute-start.4 = (f32[1,32,1024]{2,1,0:T(8,128)}, f32[1,32,1024]{2,1,0:T(8,128)}, u32[]{:S(2)}, u32[]{:S(2)}) collective-permute-start(f32[1,32,1024]{2,1,0:T(8,128)} %get-tuple-element.18), channel_id=1, source_target_pairs={{1,0},{2,1},{3,2},{4,3},{5,4},{6,5},{7,6},{9,8},{10,9},{11,10},{12... | collective-permute-start | bytes 393224 | tf_op jit(solution)/shard_map/ppermute | solution.py:22
  42.8 9.0 %collective-permute-start.5 = (f32[1,32,1024]{2,1,0:T(8,128)}, f32[1,32,1024]{2,1,0:T(8,128)}, u32[]{:S(2)}, u32[]{:S(2)}) collective-permute-start(f32[1,32,1024]{2,1,0:T(8,128)} %get-tuple-element.17), channel_id=1, source_target_pairs={{0,1},{1,2},{2,3},{3,4},{4,5},{5,6},{6,7},{8,9},{9,10},{10,11},{11... | collective-permute-start | bytes 393224 | tf_op jit(solution)/shard_map/ppermute | solution.py:20
  48.1 19.2 %all-to-all-start = ((f32[8,16,128]{2,1,0:T(8,128)}), f32[8,16,128]{2,1,0:T(8,128)S(1)}, u32[]{:S(2)}, u32[]{:S(2)}) async-start(f32[8,16,128]{2,1,0:T(8,128)} %fusion.37), calls=%async_computation | async-start | bytes 131072 | tf_op jit(solution)/shard_map/all_to_all | solution.py:44
  51.8 2.4 %copy-start.5 = (f32[16,32,1024]{2,1,0:T(8,128)S(1)}, f32[16,32,1024]{2,1,0:T(8,128)}, u32[]{:S(2)}) copy-start(f32[16,32,1024]{2,1,0:T(8,128)} %copy-done.4) | copy-start | bytes 6291460
  51.8 2.6 %copy-start.10 = (bf16[1,16,32,1024]{3,2,1,0:T(8,128)(2,1)S(1)}, bf16[1,16,32,1024]{3,2,1,0:T(8,128)(2,1)}, u32[]{:S(2)}) copy-start(bf16[1,16,32,1024]{3,2,1,0:T(8,128)(2,1)} %param.8) | copy-start | bytes 3145732
  54.4 12.3 %copy-start.18 = (s32[1,256]{1,0:T(1,128)S(1)}, s32[1,256]{1,0:T(1,128)}, u32[]{:S(2)}) copy-start(s32[1,256]{1,0:T(1,128)} %param.11) | copy-start | bytes 3076
  61.1 18.2 %collective-permute-start.6 = (f32[1,32,1024]{2,1,0:T(8,128)}, f32[1,32,1024]{2,1,0:T(8,128)}, u32[]{:S(2)}, u32[]{:S(2)}) collective-permute-start(f32[1,32,1024]{2,1,0:T(8,128)} %get-tuple-element.16), channel_id=1, source_target_pairs={{1,0},{2,1},{3,2},{4,3},{5,4},{6,5},{7,6},{9,8},{10,9},{11,10},{12... | collective-permute-start | bytes 393224 | tf_op jit(solution)/shard_map/ppermute | solution.py:22
  63.0 16.3 %collective-permute-start.7 = (f32[1,32,1024]{2,1,0:T(8,128)}, f32[1,32,1024]{2,1,0:T(8,128)}, u32[]{:S(2)}, u32[]{:S(2)}) collective-permute-start(f32[1,32,1024]{2,1,0:T(8,128)} %get-tuple-element.15), channel_id=1, source_target_pairs={{0,1},{1,2},{2,3},{3,4},{4,5},{5,6},{6,7},{8,9},{9,10},{10,11},{11... | collective-permute-start | bytes 393224 | tf_op jit(solution)/shard_map/ppermute | solution.py:20
  68.0 40.4 %all-to-all-start.1 = ((f32[32,16,128]{2,1,0:T(8,128)}), f32[32,16,128]{2,1,0:T(8,128)}, u32[]{:S(2)}, u32[]{:S(2)}) async-start(f32[32,16,128]{2,1,0:T(8,128)} %broadcast_in_dim.51), calls=%async_computation.1 | async-start | bytes 524288 | tf_op jit(solution)/shard_map/all_to_all | solution.py:38
  79.3 2.4 %copy-start.3 = (f32[16,32,1024]{2,1,0:T(8,128)S(1)}, f32[16,32,1024]{2,1,0:T(8,128)}, u32[]{:S(2)}) copy-start(f32[16,32,1024]{2,1,0:T(8,128)} %copy-done.2) | copy-start | bytes 6291460
  79.4 2.6 %copy-start.11 = (bf16[1,16,32,1024]{3,2,1,0:T(8,128)(2,1)S(1)}, bf16[1,16,32,1024]{3,2,1,0:T(8,128)(2,1)}, u32[]{:S(2)}) copy-start(bf16[1,16,32,1024]{3,2,1,0:T(8,128)(2,1)} %param.8) | copy-start | bytes 3145732
  81.9 11.8 %copy-start.22 = (s32[256,1]{0,1:T(1,128)S(1)}, s32[256,1]{0,1:T(1,128)}, u32[]{:S(2)}) copy-start(s32[256,1]{0,1:T(1,128)} %compare_select_fusion.1) | copy-start | bytes 3076
  81.9 31.5 %copy-start.19 = (s32[1,256]{1,0:T(1,128)S(1)}, s32[1,256]{1,0:T(1,128)}, u32[]{:S(2)}) copy-start(s32[1,256]{1,0:T(1,128)} %param.11) | copy-start | bytes 3076
  81.9 31.5 %copy-start.21 = (f32[1,256]{1,0:T(1,128)S(1)}, f32[1,256]{1,0:T(1,128)}, u32[]{:S(2)}) copy-start(f32[1,256]{1,0:T(1,128)} %param.10) | copy-start | bytes 3076
  88.5 6.5 %collective-permute-start.8 = (f32[1,256]{1,0:T(1,128)S(1)}, f32[1,256]{1,0:T(1,128)S(1)}, u32[]{:S(2)}, u32[]{:S(2)}) collective-permute-start(f32[1,256]{1,0:T(1,128)S(1)} %div.18), channel_id=1, source_target_pairs={{0,128},{8,136},{16,144},{24,152},{32,160},{40,168},{48,176},{56,1... | collective-permute-start | bytes 3080 | tf_op jit(solution)/shard_map/ppermute | solution.py:32
  110.0 8.3 %all-to-all-start.2 = ((f32[8,16,128]{2,1,0:T(8,128)}), f32[8,16,128]{2,1,0:T(8,128)S(1)}, u32[]{:S(2)}, u32[]{:S(2)}) async-start(f32[8,16,128]{2,1,0:T(8,128)} %broadcast_in_dim.52), calls=%async_computation.2 | async-start | bytes 131072 | tf_op jit(solution)/shard_map/all_to_all | solution.py:47
  119.0 35.4 %all-to-all-start.3 = ((f32[256,1,128]{2,1,0:T(1,128)}), f32[256,1,128]{2,1,0:T(1,128)S(1)}, u32[]{:S(2)}, u32[]{:S(2)}) async-start(f32[256,1,128]{2,1,0:T(1,128)} %broadcast_in_dim.54), calls=%async_computation.3 | async-start | bytes 262144 | tf_op jit(solution)/shard_map/all_to_all | solution.py:38
  (4 other events, 4.0 us)
where the time goes:
time: 156 us
  starting transfers between devices  59.9 us (38%)
  other arithmetic  56.9 us (36%)
  local copies, waits for them, and re-layouts  16.7 us (11%)
  blocking collectives  11.7 us (8%)
  waiting for transfers between devices  7.42 us (5%)
  matrix products  1.95 us (1%)
    all_to_all x2, starting transfers between devices, gather_sum(): return jnp.sum(lax.all_to_all(copies, axes, 0, 0, tiled=True), axis=0)  22.6 us
    add x4, other arithmetic, march_forward(): centre + STEP_SIZE * (diffuse_subdomain.astype(jnp.float32) * spread - ca...  21.2 us
    ppermute x4, starting transfers between devices, padded(): lax.ppermute(tail, axis, [(i, (i + 1) % count) for i in range(ends)])  13.4 us
    another operation x3, other arithmetic, shards(): lower_factor = jnp.linalg.cholesky(gram_matrix)  12.4 us
    all_gather x1, blocking collectives, shards(): partner_all = lax.all_gather(partner_own, 'slab', axis=1, tiled=True)  11.7 us
    ppermute x4, starting transfers between devices, padded(): lax.ppermute(head, axis, [((i + 1) % count, i) for i in range(ends)])  11.4 us
    another operation x2, other arithmetic, shards(): lax.linalg.triangular_solve(lower_factor, half_solve, left_side=True, low...  10.5 us
    concatenate x4, other arithmetic, surround_wrapper(): jnp.concatenate([bottom, block_rows, mirror_layer[:, None, :]], axis=1)  9.12 us
  transfers between devices with their start and end apart: 13, of which 4 were waited for; matrix products, arithmetic and copies ran while one was open for 30% of the time, Pallas kernels for 0%

commit v1 on v0

--- a/solution.py
+++ b/solution.py
@@ -117,7 +117,9 @@
     face_means = face_means.reshape(1, rows_dev)
     top_bit = lax.axis_size("wide").bit_length() - 2
     partner_own = partner(face_means, "wide", top_bit)
-    partner_all = lax.all_gather(partner_own, "slab", axis=1, tiled=True)
+    partner_all = jnp.concatenate(
+        lax.all_to_all(jnp.stack([partner_own] * lax.axis_size("slab")), "slab", 0, 0), axis=1
+    )
     tilde = jnp.take(partner_all[0], partner_facing_rows[0], axis=0)
     resid = tilde - interface_guess[0]
     proj_local = jnp.dot(

time: 156 us -> 160 us (1.026)
  waiting for transfers between devices: 7.42 us -> 23.1 us
  blocking collectives: 11.7 us -> 0 us
  starting transfers between devices: 59.9 us -> 63.3 us
  other arithmetic: 56.9 us -> 54.3 us
    all_gather x1 -> x0, blocking collectives: 11.7 us -> none  [shards(): partner_all = lax.all_gather(partner_own, 'slab', axis=1, tiled=True)]
    all_to_all x2, waiting for transfers between devices: 0.01 us -> 9.44 us  [gather_sum(): return jnp.sum(lax.all_to_all(copies, axes, 0, 0, tiled=True), axis=0)]
    all_to_all x2, starting transfers between devices: 22.6 us -> 15.7 us  [gather_sum(): return jnp.sum(lax.all_to_all(copies, axes, 0, 0, tiled=True), axis=0)]
    all_to_all x0 -> x1, starting transfers between devices: none -> 5.67 us  [shards(): lax.all_to_all(jnp.stack([partner_own] * lax.axis_size('slab')), 'slab',...]
    all_to_all x0 -> x1, waiting for transfers between devices: none -> 4.6 us  [shards(): lax.all_to_all(jnp.stack([partner_own] * lax.axis_size('slab')), 'slab',...]
    all_to_all x1, starting transfers between devices: 3.44 us -> 5.69 us  [sum_everywhere(): lax.all_to_all(copies, 'slab', 0, 0, tiled=True).reshape(square.shape)]
    concatenate x4, other arithmetic: 9.12 us -> 7.44 us  [surround_wrapper(): jnp.concatenate([bottom, block_rows, mirror_layer[:, None, :]], axis=1)]
    ppermute x1, starting transfers between devices: 5.28 us -> 6.94 us  [partner(): return lax.ppermute(value, axis, pairs)]
  transfers between devices with their start and end apart: 13 -> 14, of which waited for: 4 -> 8; matrix products, arithmetic and copies ran while one was open for 30% -> 23% of each run, Pallas kernels for 0% -> 0%
where the time goes in v1:
time: 160 us; the launch traced here: 159 us
  starting transfers between devices  63.3 us (40%)
  other arithmetic  54.3 us (34%)
  waiting for transfers between devices  23.1 us (14%)
  local copies, waits for them, and re-layouts  15.1 us (9%)
  matrix products  1.95 us (1%)
    add x4, other arithmetic, march_forward(): centre + STEP_SIZE * (diffuse_subdomain.astype(jnp.float32) * spread - ca...  21.8 us
    all_to_all x2, starting transfers between devices, gather_sum(): return jnp.sum(lax.all_to_all(copies, axes, 0, 0, tiled=True), axis=0)  15.7 us
    ppermute x4, starting transfers between devices, padded(): lax.ppermute(tail, axis, [(i, (i + 1) % count) for i in range(ends)])  14.2 us
    another operation x3, other arithmetic, shards(): lower_factor = jnp.linalg.cholesky(gram_matrix)  12.4 us
    ppermute x4, starting transfers between devices, padded(): lax.ppermute(head, axis, [((i + 1) % count, i) for i in range(ends)])  11.4 us
    another operation x2, other arithmetic, shards(): lax.linalg.triangular_solve(lower_factor, half_solve, left_side=True, low...  10.5 us
    all_to_all x2, waiting for transfers between devices, gather_sum(): return jnp.sum(lax.all_to_all(copies, axes, 0, 0, tiled=True), axis=0)  9.44 us
    unnamed x35, local copies, waits for them, and re-layouts  7.45 us
  transfers between devices with their start and end apart: 14, of which 8 were waited for; matrix products, arithmetic and copies ran while one was open for 23% of the time, Pallas kernels for 0%

profile of v1, /device:TPU:1, one launch (start us, length us, event | category | flops | bytes accessed | tf_op | source)
XLA Modules:
  0.0 158.8 jit_solution(14438123083305958050)
XLA Ops:
  1.7 5.1 %collective-permute-start = (f32[1,32,1024]{2,1,0:T(8,128)S(1)}, f32[1,32,1024]{2,1,0:T(8,128)S(1)}, u32[]{:S(2)}, u32[]{:S(2)}) collective-permute-start(f32[1,32,1024]{2,1,0:T(8,128)S(1)} %get-tuple-element.22), channel_id=1, source_target_pairs={{1,0},{2,1},{3,2},{4,3},{5,4},{6,5},{7,6},{9,8},{10,9},{11,10},{12... | collective-permute-start | bytes 393224 | tf_op jit(solution)/shard_map/ppermute | solution.py:22
  6.8 1.9 %collective-permute-start.1 = (f32[1,32,1024]{2,1,0:T(8,128)S(1)}, f32[1,32,1024]{2,1,0:T(8,128)S(1)}, u32[]{:S(2)}, u32[]{:S(2)}) collective-permute-start(f32[1,32,1024]{2,1,0:T(8,128)S(1)} %get-tuple-element.21), channel_id=1, source_target_pairs={{0,1},{1,2},{2,3},{3,4},{4,5},{5,6},{6,7},{8,9},{9,10},{10,11},{11... | collective-permute-start | bytes 393224 | tf_op jit(solution)/shard_map/ppermute | solution.py:20
  9.3 1.3 reduce.12
  11.7 2.3 %pad_maximum_fusion.3 = f32[18,34,1024]{2,1,0:T(8,128)S(1)} fusion(f32[18,1,1024]{2,1,0:T(1,128)S(1)} %broadcast_in_dim.48, f32[1,32,1024]{2,1,0:T(8,128)S(1)} %collective-permute-done, f32[16,32,1024]{2,1,0:T(8,128)} %bitcast.103, f32[1,32,1024]{2,1,0:T(8,128)} %copy-done.11, f32[34]{0:T(128)S(1)} %pad.74.clone), kind=kLoop, calls=%fused_computation.4 | loop fusion | flops 2506752 | bytes 4939912 | tf_op jit(solution)/shard_map/concatenate | solution.py:52
  14.5 7.0 %fusion.2 = f32[16,32,1024]{2,1,0:T(8,128)S(1)} fusion(f32[16,32,1024]{2,1,0:T(8,128)} %bitcast.104, f32[18,34,1024]{2,1,0:T(8,128)S(1)} %pad_maximum_fusion.3, f32[1,32,1024]{2,1,0:T(8,128)S(1)} %collective-permute-done, f32[1,32,1024]{2,1,0:T(8,128)S(1)} %copy-done.12, f32[18,1,1024]{2,1,0:T(1,128)S(1)} %broadcast_in_dim.48, ...), kind=kLoop, calls=%fused_computation.35 | loop fusion | flops 18874368 | bytes 11231232 | tf_op jit(solution)/shard_map/add | solution.py:78
  21.5 2.4 %collective-permute-start.2 = (f32[1,32,1024]{2,1,0:T(8,128)S(1)}, f32[1,32,1024]{2,1,0:T(8,128)S(1)}, u32[]{:S(2)}, u32[]{:S(2)}) collective-permute-start(f32[1,32,1024]{2,1,0:T(8,128)S(1)} %get-tuple-element.20), channel_id=1, source_target_pairs={{1,0},{2,1},{3,2},{4,3},{5,4},{6,5},{7,6},{9,8},{10,9},{11,10},{12... | collective-permute-start | bytes 393224 | tf_op jit(solution)/shard_map/ppermute | solution.py:22
  24.0 3.5 %collective-permute-start.3 = (f32[1,32,1024]{2,1,0:T(8,128)S(1)}, f32[1,32,1024]{2,1,0:T(8,128)S(1)}, u32[]{:S(2)}, u32[]{:S(2)}) collective-permute-start(f32[1,32,1024]{2,1,0:T(8,128)S(1)} %get-tuple-element.19), channel_id=1, source_target_pairs={{0,1},{1,2},{2,3},{3,4},{4,5},{5,6},{6,7},{8,9},{9,10},{10,11},{11... | collective-permute-start | bytes 393224 | tf_op jit(solution)/shard_map/ppermute | solution.py:20
  30.1 5.4 %fusion.5 = f32[16,32,1024]{2,1,0:T(8,128)S(1)} fusion(f32[16,32,1024]{2,1,0:T(8,128)S(1)} %fusion.2, f32[18,34,1024]{2,1,0:T(8,128)S(1)} %pad_maximum_fusion.2, f32[1,32,1024]{2,1,0:T(8,128)S(1)} %collective-permute-done.2, f32[1,32,1024]{2,1,0:T(8,128)S(1)} %collective-permute-done.3, f32[18,1,1024]{2,1,0:T(1,128)S(1)} %broadcast_in_dim.48, ...), kind=kLoop, calls=%fused_computation.38 | loop fusion | flops 18874368 | bytes 11231232 | tf_op jit(solution)/shard_map/add | solution.py:78
  35.5 1.3 copy-done.4
  37.6 1.9 %collective-permute-start.4 = (f32[1,32,1024]{2,1,0:T(8,128)}, f32[1,32,1024]{2,1,0:T(8,128)}, u32[]{:S(2)}, u32[]{:S(2)}) collective-permute-start(f32[1,32,1024]{2,1,0:T(8,128)} %get-tuple-element.18), channel_id=1, source_target_pairs={{1,0},{2,1},{3,2},{4,3},{5,4},{6,5},{7,6},{9,8},{10,9},{11,10},{12... | collective-permute-start | bytes 393224 | tf_op jit(solution)/shard_map/ppermute | solution.py:22
  39.5 4.4 %collective-permute-start.5 = (f32[1,32,1024]{2,1,0:T(8,128)}, f32[1,32,1024]{2,1,0:T(8,128)}, u32[]{:S(2)}, u32[]{:S(2)}) collective-permute-start(f32[1,32,1024]{2,1,0:T(8,128)} %get-tuple-element.17), channel_id=1, source_target_pairs={{0,1},{1,2},{2,3},{3,4},{4,5},{5,6},{6,7},{8,9},{9,10},{10,11},{11... | collective-permute-start | bytes 393224 | tf_op jit(solution)/shard_map/ppermute | solution.py:20
  44.9 1.2 collective-permute-done.5
  46.1 2.2 %pad_maximum_fusion.1 = f32[18,34,1024]{2,1,0:T(8,128)S(1)} fusion(f32[18,1,1024]{2,1,0:T(1,128)S(1)} %broadcast_in_dim.48, f32[1,32,1024]{2,1,0:T(8,128)} %collective-permute-done.4, f32[16,32,1024]{2,1,0:T(8,128)} %copy-done.4, f32[1,32,1024]{2,1,0:T(8,128)} %collective-permute-done.5, f32[34]{0:T(128)S(1)} %pad.74.clone), kind=kLoop, calls=%fused_computation.2 | loop fusion | flops 2506752 | bytes 4939912 | tf_op jit(solution)/shard_map/concatenate | solution.py:52
  48.3 4.7 %fusion.8 = f32[16,32,1024]{2,1,0:T(8,128)S(1)} fusion(f32[16,32,1024]{2,1,0:T(8,128)S(1)} %copy-done.5, f32[18,34,1024]{2,1,0:T(8,128)S(1)} %pad_maximum_fusion.1, f32[1,32,1024]{2,1,0:T(8,128)} %collective-permute-done.4, f32[1,32,1024]{2,1,0:T(8,128)} %collective-permute-done.5, f32[18,1,1024]{2,1,0:T(1,128)S(1)} %broadcast_in_dim.48, ...), kind=kLoop, calls=%fused_computation.41 | loop fusion | flops 18874368 | bytes 11231232 | tf_op jit(solution)/shard_map/add | solution.py:78
  53.1 1.3 copy-done.2
  55.1 1.9 %collective-permute-start.6 = (f32[1,32,1024]{2,1,0:T(8,128)}, f32[1,32,1024]{2,1,0:T(8,128)}, u32[]{:S(2)}, u32[]{:S(2)}) collective-permute-start(f32[1,32,1024]{2,1,0:T(8,128)} %get-tuple-element.16), channel_id=1, source_target_pairs={{1,0},{2,1},{3,2},{4,3},{5,4},{6,5},{7,6},{9,8},{10,9},{11,10},{12... | collective-permute-start | bytes 393224 | tf_op jit(solution)/shard_map/ppermute | solution.py:22
  57.0 4.4 %collective-permute-start.7 = (f32[1,32,1024]{2,1,0:T(8,128)}, f32[1,32,1024]{2,1,0:T(8,128)}, u32[]{:S(2)}, u32[]{:S(2)}) collective-permute-start(f32[1,32,1024]{2,1,0:T(8,128)} %get-tuple-element.15), channel_id=1, source_target_pairs={{0,1},{1,2},{2,3},{3,4},{4,5},{5,6},{6,7},{8,9},{9,10},{10,11},{11... | collective-permute-start | bytes 393224 | tf_op jit(solution)/shard_map/ppermute | solution.py:20
  62.3 3.7 %all-to-all-start.1 = ((f32[8,16,128]{2,1,0:T(8,128)}), f32[8,16,128]{2,1,0:T(8,128)S(1)}, u32[]{:S(2)}, u32[]{:S(2)}) async-start(f32[8,16,128]{2,1,0:T(8,128)} %fusion.37), calls=%async_computation.1 | async-start | bytes 131072 | tf_op jit(solution)/shard_map/all_to_all | solution.py:44
  66.0 2.3 %pad_maximum_fusion = f32[18,34,1024]{2,1,0:T(8,128)S(1)} fusion(f32[18,1,1024]{2,1,0:T(1,128)S(1)} %broadcast_in_dim.48, f32[1,32,1024]{2,1,0:T(8,128)} %collective-permute-done.6, f32[16,32,1024]{2,1,0:T(8,128)} %copy-done.2, f32[1,32,1024]{2,1,0:T(8,128)} %collective-permute-done.7, f32[34]{0:T(128)S(1)} %pad.74.clone), kind=kLoop, calls=%fused_computation.1 | loop fusion | flops 2506752 | bytes 4939912 | tf_op jit(solution)/shard_map/concatenate | solution.py:52
  68.6 4.7 %fusion.11 = f32[16,32,1024]{2,1,0:T(8,128)S(1)} fusion(f32[16,32,1024]{2,1,0:T(8,128)S(1)} %copy-done.3, f32[18,34,1024]{2,1,0:T(8,128)S(1)} %pad_maximum_fusion, f32[1,32,1024]{2,1,0:T(8,128)} %collective-permute-done.6, f32[1,32,1024]{2,1,0:T(8,128)} %collective-permute-done.7, f32[18,1,1024]{2,1,0:T(1,128)S(1)} %broadcast_in_dim.48, ...), kind=kLoop, calls=%fused_computation.44 | loop fusion | flops 18874368 | bytes 11231232 | tf_op jit(solution)/shard_map/add | solution.py:78
  73.3 1.3 copy-done.9
  75.1 6.9 %collective-permute-start.8 = (f32[1,256]{1,0:T(1,128)S(1)}, f32[1,256]{1,0:T(1,128)S(1)}, u32[]{:S(2)}, u32[]{:S(2)}) collective-permute-start(f32[1,256]{1,0:T(1,128)S(1)} %div.18), channel_id=1, source_target_pairs={{0,128},{8,136},{16,144},{24,152},{32,160},{40,168},{48,176},{56,1... | collective-permute-start | bytes 3080 | tf_op jit(solution)/shard_map/ppermute | solution.py:32
  83.6 5.7 %all-to-all-start = ((f32[8,1,256]{2,1,0:T(1,128)}), f32[8,1,256]{2,1,0:T(1,128)S(1)}, u32[]{:S(2)}, u32[]{:S(2)}) async-start(f32[8,1,256]{2,1,0:T(1,128)} %stack.2), calls=%async_computation | async-start | bytes 16384 | tf_op jit(solution)/shard_map/all_to_all | solution.py:121
  89.3 4.6 %all-to-all-done = f32[8,1,256]{2,1,0:T(1,128)S(1)} async-done(((f32[8,1,256]{2,1,0:T(1,128)}), f32[8,1,256]{2,1,0:T(1,128)S(1)}, u32[]{:S(2)}, u32[]{:S(2)}) %all-to-all-start) | async-done | bytes 8224 | tf_op jit(solution)/shard_map/all_to_all | solution.py:121
  94.6 9.9 %all-to-all-start.2 = ((f32[32,16,128]{2,1,0:T(8,128)}), f32[32,16,128]{2,1,0:T(8,128)S(1)}, u32[]{:S(2)}, u32[]{:S(2)}) async-start(f32[32,16,128]{2,1,0:T(8,128)} %broadcast_in_dim.51), calls=%async_computation.2 | async-start | bytes 524288 | tf_op jit(solution)/shard_map/all_to_all | solution.py:38
  104.6 1.7 %gather_fusion = f32[256]{0:T(256)S(1)} fusion(f32[2048]{0:T(1024)S(1)} %bitcast.102, s32[1024]{0:T(1024)S(1)} %pad_clamp_fusion), kind=kCustom, calls=%fused_computation | custom fusion | bytes 3072 | tf_op jit(solution)/shard_map/jit(_take)/gather | solution.py:123
  106.3 9.4 %all-to-all-done.2 = f32[32,16,128]{2,1,0:T(8,128)S(1)} async-done(((f32[32,16,128]{2,1,0:T(8,128)}), f32[32,16,128]{2,1,0:T(8,128)S(1)}, u32[]{:S(2)}, u32[]{:S(2)}) %all-to-all-start.2) | async-done | bytes 262176 | tf_op jit(solution)/shard_map/all_to_all | solution.py:38
  116.4 5.7 %all-to-all-start.3 = ((f32[8,16,128]{2,1,0:T(8,128)}), f32[8,16,128]{2,1,0:T(8,128)S(1)}, u32[]{:S(2)}, u32[]{:S(2)}) async-start(f32[8,16,128]{2,1,0:T(8,128)} %broadcast_in_dim.52), calls=%async_computation.3 | async-start | bytes 131072 | tf_op jit(solution)/shard_map/all_to_all | solution.py:47
  122.3 4.7 %all-to-all-done.3 = f32[8,16,128]{2,1,0:T(8,128)S(1)} async-done(((f32[8,16,128]{2,1,0:T(8,128)}), f32[8,16,128]{2,1,0:T(8,128)S(1)}, u32[]{:S(2)}, u32[]{:S(2)}) %all-to-all-start.3) | async-done | bytes 65568 | tf_op jit(solution)/shard_map/all_to_all | solution.py:47
  127.7 5.8 %all-to-all-start.4 = ((f32[256,1,128]{2,1,0:T(1,128)}), f32[256,1,128]{2,1,0:T(1,128)S(1)}, u32[]{:S(2)}, u32[]{:S(2)}) async-start(f32[256,1,128]{2,1,0:T(1,128)} %broadcast_in_dim.54), calls=%async_computation.4 | async-start | bytes 262144 | tf_op jit(solution)/shard_map/all_to_all | solution.py:38
  133.6 11.7 %cholesky.16 = f32[128,128]{1,0:T(8,128)S(1)} custom-call(f32[128,128]{1,0:T(8,128)S(1)} %fusion.45), custom_call_target="Cholesky" | custom-call | tf_op jit(solution)/shard_map/jit(cholesky)/cholesky | solution.py:130
  146.7 9.8 %custom-call.10 = f32[1,128,128]{1,2,0:T(8,128)S(1)} custom-call(f32[1,128,128]{2,1,0:T(8,128)S(1)} %fusion.41), custom_call_target="InvertDiagBlocksLowerTriangular" | custom-call | tf_op jit(solution)/shard_map/triangular_solve | solution.py:134
  (79 shorter events, 17.4 us)
Async XLA Ops:
  0.6 157.3 %copy-start = (f32[1,256,128]{2,1,0:T(8,128)S(1)}, f32[1,256,128]{2,1,0:T(8,128)}, u32[]{:S(2)}) copy-start(f32[1,256,128]{2,1,0:T(8,128)} %param.13) | copy-start | bytes 393220
  1.7 9.3 %collective-permute-start = (f32[1,32,1024]{2,1,0:T(8,128)S(1)}, f32[1,32,1024]{2,1,0:T(8,128)S(1)}, u32[]{:S(2)}, u32[]{:S(2)}) collective-permute-start(f32[1,32,1024]{2,1,0:T(8,128)S(1)} %get-tuple-element.22), channel_id=1, source_target_pairs={{1,0},{2,1},{3,2},{4,3},{5,4},{6,5},{7,6},{9,8},{10,9},{11,10},{12... | collective-permute-start | bytes 393224 | tf_op jit(solution)/shard_map/ppermute | solution.py:22
  6.8 4.2 %collective-permute-start.1 = (f32[1,32,1024]{2,1,0:T(8,128)S(1)}, f32[1,32,1024]{2,1,0:T(8,128)S(1)}, u32[]{:S(2)}, u32[]{:S(2)}) collective-permute-start(f32[1,32,1024]{2,1,0:T(8,128)S(1)} %get-tuple-element.21), channel_id=1, source_target_pairs={{0,1},{1,2},{2,3},{3,4},{4,5},{5,6},{6,7},{8,9},{9,10},{10,11},{11... | collective-permute-start | bytes 393224 | tf_op jit(solution)/shard_map/ppermute | solution.py:20
  11.0 0.7 copy-start.11
  11.7 2.6 %copy-start.1 = (bf16[3,1,16,32,1024]{4,3,2,1,0:T(8,128)(2,1)S(1)}, bf16[3,1,16,32,1024]{4,3,2,1,0:T(8,128)(2,1)}, u32[]{:S(2)}) copy-start(bf16[3,1,16,32,1024]{4,3,2,1,0:T(8,128)(2,1)} %param.9) | copy-start | bytes 9437188
  11.7 2.8 %copy-start.6 = (bf16[1,16,32,1024]{3,2,1,0:T(8,128)(2,1)S(1)}, bf16[1,16,32,1024]{3,2,1,0:T(8,128)(2,1)}, u32[]{:S(2)}) copy-start(bf16[1,16,32,1024]{3,2,1,0:T(8,128)(2,1)} %param.8) | copy-start | bytes 3145732
  11.7 2.8 %copy-start.12 = (f32[1,32,1024]{2,1,0:T(8,128)S(1)}, f32[1,32,1024]{2,1,0:T(8,128)}, u32[]{:S(2)}) copy-start(f32[1,32,1024]{2,1,0:T(8,128)} %copy-done.11) | copy-start | bytes 393220
  21.5 6.7 %collective-permute-start.2 = (f32[1,32,1024]{2,1,0:T(8,128)S(1)}, f32[1,32,1024]{2,1,0:T(8,128)S(1)}, u32[]{:S(2)}, u32[]{:S(2)}) collective-permute-start(f32[1,32,1024]{2,1,0:T(8,128)S(1)} %get-tuple-element.20), channel_id=1, source_target_pairs={{1,0},{2,1},{3,2},{4,3},{5,4},{6,5},{7,6},{9,8},{10,9},{11,10},{12... | collective-permute-start | bytes 393224 | tf_op jit(solution)/shard_map/ppermute | solution.py:22
  24.0 5.5 %collective-permute-start.3 = (f32[1,32,1024]{2,1,0:T(8,128)S(1)}, f32[1,32,1024]{2,1,0:T(8,128)S(1)}, u32[]{:S(2)}, u32[]{:S(2)}) collective-permute-start(f32[1,32,1024]{2,1,0:T(8,128)S(1)} %get-tuple-element.19), channel_id=1, source_target_pairs={{0,1},{1,2},{2,3},{3,4},{4,5},{5,6},{6,7},{8,9},{9,10},{10,11},{11... | collective-permute-start | bytes 393224 | tf_op jit(solution)/shard_map/ppermute | solution.py:20
  30.1 13.8 %copy-start.10 = (f32[1,256,128]{2,1,0:T(8,128)S(1)}, f32[1,256,128]{2,1,0:T(8,128)}, u32[]{:S(2)}) copy-start(f32[1,256,128]{2,1,0:T(8,128)} %param.12) | copy-start | bytes 393220
  35.5 1.3 copy-start.4
  37.6 7.3 %collective-permute-start.4 = (f32[1,32,1024]{2,1,0:T(8,128)}, f32[1,32,1024]{2,1,0:T(8,128)}, u32[]{:S(2)}, u32[]{:S(2)}) collective-permute-start(f32[1,32,1024]{2,1,0:T(8,128)} %get-tuple-element.18), channel_id=1, source_target_pairs={{1,0},{2,1},{3,2},{4,3},{5,4},{6,5},{7,6},{9,8},{10,9},{11,10},{12... | collective-permute-start | bytes 393224 | tf_op jit(solution)/shard_map/ppermute | solution.py:22
  39.5 6.6 %collective-permute-start.5 = (f32[1,32,1024]{2,1,0:T(8,128)}, f32[1,32,1024]{2,1,0:T(8,128)}, u32[]{:S(2)}, u32[]{:S(2)}) collective-permute-start(f32[1,32,1024]{2,1,0:T(8,128)} %get-tuple-element.17), channel_id=1, source_target_pairs={{0,1},{1,2},{2,3},{3,4},{4,5},{5,6},{6,7},{8,9},{9,10},{10,11},{11... | collective-permute-start | bytes 393224 | tf_op jit(solution)/shard_map/ppermute | solution.py:20
  44.6 3.7 %copy-start.5 = (f32[16,32,1024]{2,1,0:T(8,128)S(1)}, f32[16,32,1024]{2,1,0:T(8,128)}, u32[]{:S(2)}) copy-start(f32[16,32,1024]{2,1,0:T(8,128)} %copy-done.4) | copy-start | bytes 6291460
  44.6 3.7 %copy-start.7 = (bf16[1,16,32,1024]{3,2,1,0:T(8,128)(2,1)S(1)}, bf16[1,16,32,1024]{3,2,1,0:T(8,128)(2,1)}, u32[]{:S(2)}) copy-start(bf16[1,16,32,1024]{3,2,1,0:T(8,128)(2,1)} %param.8) | copy-start | bytes 3145732
  48.3 13.1 %copy-start.13 = (f32[1,256,128]{1,2,0:T(8,128)S(1)}, f32[1,256,128]{1,2,0:T(8,128)}, u32[]{:S(2)}) copy-start(f32[1,256,128]{1,2,0:T(8,128)} %copy.21) | copy-start | bytes 393220
  53.0 1.3 copy-start.2
  55.1 10.9 %collective-permute-start.6 = (f32[1,32,1024]{2,1,0:T(8,128)}, f32[1,32,1024]{2,1,0:T(8,128)}, u32[]{:S(2)}, u32[]{:S(2)}) collective-permute-start(f32[1,32,1024]{2,1,0:T(8,128)} %get-tuple-element.16), channel_id=1, source_target_pairs={{1,0},{2,1},{3,2},{4,3},{5,4},{6,5},{7,6},{9,8},{10,9},{11,10},{12... | collective-permute-start | bytes 393224 | tf_op jit(solution)/shard_map/ppermute | solution.py:22
  57.0 9.0 %collective-permute-start.7 = (f32[1,32,1024]{2,1,0:T(8,128)}, f32[1,32,1024]{2,1,0:T(8,128)}, u32[]{:S(2)}, u32[]{:S(2)}) collective-permute-start(f32[1,32,1024]{2,1,0:T(8,128)} %get-tuple-element.15), channel_id=1, source_target_pairs={{0,1},{1,2},{2,3},{3,4},{4,5},{5,6},{6,7},{8,9},{9,10},{10,11},{11... | collective-permute-start | bytes 393224 | tf_op jit(solution)/shard_map/ppermute | solution.py:20
  62.3 19.8 %all-to-all-start.1 = ((f32[8,16,128]{2,1,0:T(8,128)}), f32[8,16,128]{2,1,0:T(8,128)S(1)}, u32[]{:S(2)}, u32[]{:S(2)}) async-start(f32[8,16,128]{2,1,0:T(8,128)} %fusion.37), calls=%async_computation.1 | async-start | bytes 131072 | tf_op jit(solution)/shard_map/all_to_all | solution.py:44
  66.0 2.4 %copy-start.3 = (f32[16,32,1024]{2,1,0:T(8,128)S(1)}, f32[16,32,1024]{2,1,0:T(8,128)}, u32[]{:S(2)}) copy-start(f32[16,32,1024]{2,1,0:T(8,128)} %copy-done.2) | copy-start | bytes 6291460
  66.0 2.6 %copy-start.8 = (bf16[1,16,32,1024]{3,2,1,0:T(8,128)(2,1)S(1)}, bf16[1,16,32,1024]{3,2,1,0:T(8,128)(2,1)}, u32[]{:S(2)}) copy-start(bf16[1,16,32,1024]{3,2,1,0:T(8,128)(2,1)} %param.8) | copy-start | bytes 3145732
  68.6 36.0 %copy-start.14 = (s32[1,256]{1,0:T(1,128)S(1)}, s32[1,256]{1,0:T(1,128)}, u32[]{:S(2)}) copy-start(s32[1,256]{1,0:T(1,128)} %param.11) | copy-start | bytes 3076
  73.3 1.3 copy-start.9
  74.6 47.5 %copy-start.15 = (f32[1,256]{1,0:T(1,128)S(1)}, f32[1,256]{1,0:T(1,128)}, u32[]{:S(2)}) copy-start(f32[1,256]{1,0:T(1,128)} %param.10) | copy-start | bytes 3076
  75.1 7.9 %collective-permute-start.8 = (f32[1,256]{1,0:T(1,128)S(1)}, f32[1,256]{1,0:T(1,128)S(1)}, u32[]{:S(2)}, u32[]{:S(2)}) collective-permute-start(f32[1,256]{1,0:T(1,128)S(1)} %div.18), channel_id=1, source_target_pairs={{0,128},{8,136},{16,144},{24,152},{32,160},{40,168},{48,176},{56,1... | collective-permute-start | bytes 3080 | tf_op jit(solution)/shard_map/ppermute | solution.py:32
  83.6 10.3 %all-to-all-start = ((f32[8,1,256]{2,1,0:T(1,128)}), f32[8,1,256]{2,1,0:T(1,128)S(1)}, u32[]{:S(2)}, u32[]{:S(2)}) async-start(f32[8,1,256]{2,1,0:T(1,128)} %stack.2), calls=%async_computation | async-start | bytes 16384 | tf_op jit(solution)/shard_map/all_to_all | solution.py:121
  94.6 21.2 %all-to-all-start.2 = ((f32[32,16,128]{2,1,0:T(8,128)}), f32[32,16,128]{2,1,0:T(8,128)S(1)}, u32[]{:S(2)}, u32[]{:S(2)}) async-start(f32[32,16,128]{2,1,0:T(8,128)} %broadcast_in_dim.51), calls=%async_computation.2 | async-start | bytes 524288 | tf_op jit(solution)/shard_map/all_to_all | solution.py:38
  116.4 10.6 %all-to-all-start.3 = ((f32[8,16,128]{2,1,0:T(8,128)}), f32[8,16,128]{2,1,0:T(8,128)S(1)}, u32[]{:S(2)}, u32[]{:S(2)}) async-start(f32[8,16,128]{2,1,0:T(8,128)} %broadcast_in_dim.52), calls=%async_computation.3 | async-start | bytes 131072 | tf_op jit(solution)/shard_map/all_to_all | solution.py:47
  127.7 29.9 %all-to-all-start.4 = ((f32[256,1,128]{2,1,0:T(1,128)}), f32[256,1,128]{2,1,0:T(1,128)S(1)}, u32[]{:S(2)}, u32[]{:S(2)}) async-start(f32[256,1,128]{2,1,0:T(1,128)} %broadcast_in_dim.54), calls=%async_computation.4 | async-start | bytes 262144 | tf_op jit(solution)/shard_map/all_to_all | solution.py:38
